TPU v7x, 512 devices: a whole 4x4x16 slice. The times are simulated.
512 devices in a mesh: filter: 32 (over z_lo, x), space: 16 (over z_hi, y, core).
Axes of the slice: x: 4, y: 4, z: 16 (z_hi: 2, z_lo: 8; z = z_hi * 8 + z_lo), core: 2. Of those that a mesh axis runs over, the one named last changes fastest.
Arguments:
- volume: bfloat16 [1024, 64, 1024], P('filter', 'space'), may hold values from -6 to 6
- mixing: bfloat16 [1024, 1024], P('filter'), may hold values from -0.1875 to 0.1875
- kernel_taps: float32 [1024, 27], P('filter'), may hold values from -1.25 to 1.25
- upstream: bfloat16 [1024, 64, 1024], P('filter', 'space'), may hold values from -6 to 6
Outputs:
- output: bfloat16 [1024, 64, 1024], P('filter', 'space')
- volume_grad: bfloat16 [1024, 64, 1024], P('filter', 'space')
- mixing_grad: float32 [1024, 1024], P('filter', 'space')
- taps_grad: float32 [1024, 27], P('filter')
All inputs are finite; a program needn't handle non-finite values.
Results may differ from a plain program's by a relative error of at most 0.0055.
Values may be sent and summed in bfloat16 or wider, within the bound.
A program may use at most 64 MiB of HBM per device.

v0:
```python
import math

import jax
import jax.numpy as jnp
from jax import lax
from jax.sharding import PartitionSpec as P

WW = 64


def padded_2(array, sides, width):
    for axis, dim in sides:
        size, length = (lax.axis_size(axis), array.shape[dim])
        up = [(i, (i + 1) % size) for i in range(size - 1)]
        down = [(j, i) for i, j in up]
        last = lax.slice_in_dim(array, length - width, length, axis=dim)
        leading = lax.slice_in_dim(array, 0, width, axis=dim)
        before = lax.ppermute(last, axis, up)
        after = lax.ppermute(leading, axis, down)
        array = jnp.concatenate([before, array, after], axis=dim)
    return array


def pad_rows_cols(field):
    return jnp.pad(field, ((0, 0), (0, 0), (1, 1), (1, 1)))


def depth_conv(padded, kernel_taps, flip):
    depth = padded.shape[1] - 2
    height = padded.shape[2] - 2
    breadth = padded.shape[3] - 2
    summed = jnp.zeros((padded.shape[0], depth, height, breadth), jnp.float32)
    for plane_off in range(3):
        for row_off in range(3):
            for col_off in range(3):
                index_tap = plane_off * 9 + row_off * 3 + col_off
                if flip:
                    plane_at, row_at, col_at = (2 - plane_off, 2 - row_off, 2 - col_off)
                else:
                    plane_at, row_at, col_at = (plane_off, row_off, col_off)
                window = padded[
                    :,
                    plane_at : plane_at + depth,
                    row_at : row_at + height,
                    col_at : col_at + breadth,
                ]
                summed = summed + kernel_taps[:, index_tap][:, None, None, None] * window.astype(
                    jnp.float32
                )
    return summed


def tap_grads(grad_field, padded):
    depth = grad_field.shape[1]
    height = grad_field.shape[2]
    breadth = grad_field.shape[3]
    grad_wide = grad_field.astype(jnp.float32)
    columns_list = []
    for plane_off in range(3):
        for row_off in range(3):
            for col_off in range(3):
                window = padded[
                    :,
                    plane_off : plane_off + depth,
                    row_off : row_off + height,
                    col_off : col_off + breadth,
                ]
                columns_list.append(jnp.sum(grad_wide * window.astype(jnp.float32), axis=(1, 2, 3)))
    return jnp.stack(columns_list, axis=1)


def silu_slope(values):
    sig_val = jax.nn.sigmoid(values)
    return sig_val * (1.0 + values * (1.0 - sig_val))


def body(volume, mixing, kernel_taps, upstream):
    channels = volume.shape[0]
    planes = volume.shape[1]
    flat_cells = volume.shape[2]
    row_count = flat_cells // WW
    slab_cells = planes * flat_cells
    space_count = lax.axis_size("space")
    norm_factor = 1.0 / math.sqrt(planes * space_count * flat_cells)
    flat_vol = volume.reshape(channels, slab_cells)
    vol_all = lax.all_gather(flat_vol, "filter", axis=0, tiled=True)
    mixed = jnp.dot(mixing, vol_all, preferred_element_type=jnp.float32).astype(jnp.bfloat16)
    mixed_grid = mixed.reshape(channels, planes, row_count, WW)
    up_grid = upstream.reshape(channels, planes, row_count, WW)
    mixed_rim = padded_2(mixed_grid, (("space", 1),), 1)
    mixed_pad = pad_rows_cols(mixed_rim)
    spatial = depth_conv(mixed_pad, kernel_taps, False)
    grad_own = (up_grid.astype(jnp.float32) * silu_slope(spatial)).astype(jnp.bfloat16)
    grad_wide = padded_2(grad_own, (("space", 1),), 1)
    vol_grid = volume.reshape(channels, planes, row_count, WW).astype(jnp.float32)
    output = (
        (vol_grid + jax.nn.silu(spatial)).astype(jnp.bfloat16).reshape(channels, planes, flat_cells)
    )
    spatial_grad = grad_wide[:, 1:-1]
    mixed_grad = (
        depth_conv(pad_rows_cols(grad_wide), kernel_taps, True)
        .astype(jnp.bfloat16)
        .reshape(channels, slab_cells)
    )
    taps_part = tap_grads(spatial_grad, mixed_pad) * norm_factor
    taps_grad = lax.psum(taps_part, "space")
    weight_cols = lax.all_to_all(mixing, "filter", split_axis=1, concat_axis=0, tiled=True)
    back_sum = lax.dot_general(
        weight_cols,
        lax.all_gather(mixed_grad, "filter", axis=0, tiled=True),
        (((0,), (0,)), ((), ())),
        preferred_element_type=jnp.float32,
    )
    weight_term = (
        lax.dot_general(
            mixed_grad, vol_all, (((1,), (1,)), ((), ())), preferred_element_type=jnp.float32
        )
        * norm_factor
    )
    mixing_grad = lax.psum_scatter(weight_term, "space", scatter_dimension=1, tiled=True)
    volume_grad = (
        (upstream.reshape(channels, slab_cells).astype(jnp.float32) + back_sum)
        .astype(jnp.bfloat16)
        .reshape(channels, planes, flat_cells)
    )
    return (output, volume_grad, mixing_grad, taps_grad)


def solution(mesh):
    in_specs = (
        P("filter", "space", None),
        P("filter", None),
        P("filter", None),
        P("filter", "space", None),
    )
    out_specs = (
        P("filter", "space", None),
        P("filter", "space", None),
        P("filter", "space"),
        P("filter", None),
    )
    return jax.shard_map(body, mesh=mesh, in_specs=in_specs, out_specs=out_specs, check_vma=False)
```

profile of v0, /device:TPU:8, one launch (start us, length us, event | category | flops | bytes accessed | tf_op | source)
XLA Modules:
  0.0 666.5 jit_solution(4207602100597087472)
XLA Ops:
  7.2 1.7 copy.16
  9.0 1.3 reshape.69
  10.3 2.0 slice_reduce_fusion.26
  12.3 239.7 %all-gather.3.cloned.1.call-done = bf16[1024,4096]{1,0:T(8,128)(2,1)} async-done(((bf16[32,4096]{1,0:T(8,128)(2,1)}), bf16[1024,4096]{1,0:T(8,128)(2,1)}) %all-gather.3.cloned.1.call-update) | async-done | bytes 8388624 | tf_op jit(solution)/shard_map/all_gather | solution.py:86
  252.0 4.9 convolution_convert_fusion
  257.5 1.9 collective-permute-start
  259.4 3.6 collective-permute-start.1
  263.8 1.8 collective-permute-done.1
  266.4 11.5 %fusion.72 = (f32[32]{0:T(128)S(1)}, f32[32]{0:T(128)S(1)}, f32[32]{0:T(128)S(1)}, f32[32]{0:T(128)S(1)}, f32[32]{0:T(128)}, /*index=5*/f32[32]{0:T(128)}, f32[3...) fusion(bf16[32,6,18,66]{3,2,1,0:T(8,128)(2,1)S(1)} %select_maxi, ...), kind=kLoop, calls=%fused_computation.138 | loop fusion | flops 16776640 | bytes 8001152 | tf_op jit(solution)/shard_map/reduce_sum | solution.py:68
  277.9 3.6 collective-permute-start.2
  281.5 2.1 collective-permute-start.3
  284.3 1.8 collective-permute-done.3
  286.9 5.8 fusion.73
  293.2 6.1 convolution_multiply_fusion
  302.2 12.8 %all-to-all-start = ((bf16[32,2,512]{2,1,0:T(2,128)(2,1)}), bf16[32,2,512]{2,1,0:T(2,128)(2,1)}, u32[]{:S(2)}, u32[]{:S(2)}) async-start(bf16[32,2,512]{2,1,0:T(2,128)(2,1)} %reshape.99), calls=%async_computation | async-start | bytes 131072 | tf_op jit(solution)/shard_map/all_to_all | solution.py:107
  315.1 1.3 reshape.67
  317.5 10.2 %all-to-all-done = bf16[32,2,512]{2,1,0:T(2,128)(2,1)} async-done(((bf16[32,2,512]{2,1,0:T(2,128)(2,1)}), bf16[32,2,512]{2,1,0:T(2,128)(2,1)}, u32[]{:S(2)}, u32[]{:S(2)}) %all-to-all-start) | async-done | bytes 65568 | tf_op jit(solution)/shard_map/all_to_all | solution.py:107
  329.8 3.0 fusion.71
  332.8 2.9 stack.111
  335.6 112.0 %psum.7 = f32[32,27]{0,1:T(8,128)S(1)} all-reduce(f32[32,27]{0,1:T(8,128)S(1)} %broadcast_multiply_fusion), channel_id=1, replica_groups=mesh['filter'=32,'space'=16] {'space'}, use_global_device_ids=true, to_apply=%region_28.29 | all-reduce | flops 864 | bytes 6912 | tf_op jit(solution)/shard_map/psum | solution.py:106
  448.4 1.5 add_convert_fusion
  450.9 1.4 copy.15
  452.3 201.8 %all-gather.5.cloned.1.call-done = bf16[1024,4096]{1,0:T(8,128)(2,1)} async-done(((bf16[32,4096]{1,0:T(8,128)(2,1)}), bf16[1024,4096]{1,0:T(8,128)(2,1)}) %all-gather.5.cloned.1.call-update) | async-done | bytes 8388624 | tf_op jit(solution)/shard_map/all_gather | solution.py:110
  654.1 4.9 fusion.1
  (55 shorter events, 12.8 us)
Async XLA Ops:
  7.2 244.8 %copy-start.11 = (bf16[32,1024]{1,0:T(8,128)(2,1)S(1)}, bf16[32,1024]{1,0:T(8,128)(2,1)}, u32[]{:S(2)}) copy-start(bf16[32,1024]{1,0:T(8,128)(2,1)} %param.5) | copy-start | bytes 196612
  7.2 244.8 %all-gather.3.cloned.1.call-start = ((), (), s32[]{:S(2)}) async-start(), calls=%async_computation.2 | async-start | bytes 8650752 | tf_op jit(solution)/shard_map/all_gather | solution.py:86
  9.0 441.9 %reduce-scatter.4.cloned.1.call-start = ((), (), s32[]{:S(2)}) async-start(), calls=%async_computation.4 | async-start | bytes 557056
  12.3 250.8 %copy-start = (f32[32,27]{1,0:T(8,128)S(1)}, f32[32,27]{1,0:T(8,128)}, u32[]{:S(2)}) copy-start(f32[32,27]{1,0:T(8,128)} %param.6) | copy-start | bytes 10372
  257.5 6.3 collective-permute-start
  259.4 6.1 collective-permute-start.1
  263.8 14.1 %copy-start.4 = (bf16[32,1,16,64]{3,2,1,0:T(8,128)(2,1)}, bf16[32,1,16,64]{3,2,1,0:T(8,128)(2,1)S(1)}, u32[]{:S(2)}) copy-start(bf16[32,1,16,64]{3,2,1,0:T(8,128)(2,1)S(1)} %collective-permute-done) | copy-start | bytes 196612
  265.6 12.3 %copy-start.6 = (bf16[32,1,16,64]{3,2,1,0:T(8,128)(2,1)}, bf16[32,1,16,64]{3,2,1,0:T(8,128)(2,1)S(1)}, u32[]{:S(2)}) copy-start(bf16[32,1,16,64]{3,2,1,0:T(8,128)(2,1)S(1)} %collective-permute-done.1) | copy-start | bytes 196612
  277.9 6.4 collective-permute-start.2
  281.5 4.6 collective-permute-start.3
  293.2 6.1 copy-start.2
  293.2 7.9 %copy-start.12 = (bf16[32,1024]{1,0:T(8,128)(2,1)S(1)}, bf16[32,1024]{1,0:T(8,128)(2,1)}, u32[]{:S(2)}) copy-start(bf16[32,1024]{1,0:T(8,128)(2,1)} %param.5) | copy-start | bytes 196612
  299.3 15.7 %copy-start.8 = (bf16[32,4,1024]{2,1,0:T(4,128)(2,1)S(1)}, bf16[32,4,1024]{2,1,0:T(4,128)(2,1)}, u32[]{:S(2)}) copy-start(bf16[32,4,1024]{2,1,0:T(4,128)(2,1)} %param.7) | copy-start | bytes 786436
  299.3 15.8 %copy-start.9 = (bf16[32,4,1024]{2,1,0:T(4,128)(2,1)S(1)}, bf16[32,4,1024]{2,1,0:T(4,128)(2,1)}, u32[]{:S(2)}) copy-start(bf16[32,4,1024]{2,1,0:T(4,128)(2,1)} %param.4) | copy-start | bytes 786436
  300.4 353.7 %all-gather.5.cloned.1.call-start = ((), (), s32[]{:S(2)}) async-start(), calls=%async_computation.3 | async-start | bytes 8650752 | tf_op jit(solution)/shard_map/all_gather | solution.py:110
  302.2 25.5 %all-to-all-start = ((bf16[32,2,512]{2,1,0:T(2,128)(2,1)}), bf16[32,2,512]{2,1,0:T(2,128)(2,1)}, u32[]{:S(2)}, u32[]{:S(2)}) async-start(bf16[32,2,512]{2,1,0:T(2,128)(2,1)} %reshape.99), calls=%async_computation | async-start | bytes 131072 | tf_op jit(solution)/shard_map/all_to_all | solution.py:107
  315.0 14.8 %copy-start.5 = (bf16[32,1,16,64]{3,2,1,0:T(8,128)(2,1)S(1)}, bf16[32,1,16,64]{3,2,1,0:T(8,128)(2,1)}, u32[]{:S(2)}) copy-start(bf16[32,1,16,64]{3,2,1,0:T(8,128)(2,1)} %copy-done.4) | copy-start | bytes 196612
  315.0 14.8 %copy-start.7 = (bf16[32,1,16,64]{3,2,1,0:T(8,128)(2,1)S(1)}, bf16[32,1,16,64]{3,2,1,0:T(8,128)(2,1)}, u32[]{:S(2)}) copy-start(bf16[32,1,16,64]{3,2,1,0:T(8,128)(2,1)} %copy-done.6) | copy-start | bytes 196612
  329.8 118.6 %copy-start.1 = (f32[32,4,16,64]{3,2,1,0:T(8,128)S(1)}, f32[32,4,16,64]{3,2,1,0:T(8,128)}, u32[]{:S(2)}) copy-start(f32[32,4,16,64]{3,2,1,0:T(8,128)} %get-tuple-element.74) | copy-start | bytes 1572868
  332.8 321.3 %copy-start.3 = (f32[4,8,4,1024]{3,1,2,0:T(8,128)S(1)}, f32[4,8,4,1024]{3,1,2,0:T(8,128)}, u32[]{:S(2)}) copy-start(f32[4,8,4,1024]{3,1,2,0:T(8,128)} %copy.17) | copy-start | bytes 1572868
  332.8 321.3 %copy-start.10 = (bf16[1024,32]{0,1:T(8,128)(2,1)S(1)}, bf16[1024,32]{0,1:T(8,128)(2,1)}, u32[]{:S(2)}) copy-start(bf16[1024,32]{0,1:T(8,128)(2,1)} %all_to_all.17) | copy-start | bytes 196612
Sparse Core Ops, SparseCore 0:
  10.7 241.2 all-gather.2
  300.5 122.5 reduce-scatter.3
  426.0 228.1 all-gather.4
where the time goes:
time: 668 us; the launch traced here: 666 us
  waiting for transfers between devices  457 us (68%)
  blocking collectives  112 us (17%)
  starting transfers between devices  24.2 us (4%)
  other arithmetic  23.4 us (4%)
  local copies, waits for them, and re-layouts  19.8 us (3%)
  matrix products  15.9 us (2%)
  between operations  14 us (2%)
    all_gather x1, waiting for transfers between devices, body(): vol_all = lax.all_gather(flat_vol, 'filter', axis=0, tiled=True)  240 us
    all_gather x1, waiting for transfers between devices, body(): lax.all_gather(mixed_grad, 'filter', axis=0, tiled=True)  202 us
    psum x1, blocking collectives, body(): taps_grad = lax.psum(taps_part, 'space')  112 us
    reduce_sum x2, other arithmetic, tap_grads(): jnp.sum(grad_wide * window.astype(jnp.float32), axis=(1, 2, 3))  14.4 us
  transfers between devices with their start and end apart: 8, of which 7 were waited for; matrix products, arithmetic and copies ran while one was open for 3% of the time, Pallas kernels for 0%

commit v1 on v0

v1 whole, which is shorter than its diff:
```python
import functools
import math

import jax
import jax.numpy as jnp
from jax import lax
from jax.experimental import pallas as pl
from jax.experimental.pallas import tpu as pltpu
from jax.sharding import PartitionSpec as P

F32 = jnp.float32
BF16 = jnp.bfloat16
MESH = pl.DeviceIdType.MESH

NZ, NX, NY = 8, 4, 4
NF, NS = 32, 16
CH = 32
PLANES, CELLS, WW = 4, 1024, 64
SLAB = PLANES * CELLS
PART = SLAB // NZ
C = NF * CH
HALF = PART // 2
ORDER = (4, 3, 5, 2, 6, 1, 7)


class Slots:
    def __init__(self):
        self.used = 0

    def take(self, n):
        first = self.used
        self.used += n
        return first


N_SEMS = 330


def kernel(
    norm, vol, up, mix, taps, out, vgrad, mgrad, tgrad,
    vol_all, mg_all, wall, wt, mq, bq, mb, m32, sg32, sp32, sgb, sgh, mgb, bb, tb, tg, ts, tr,
    dw, d1, a1b, d2, a2, a2b, d3, d4s, d4r, sems,
):
    f = lax.axis_index("filter")
    s = lax.axis_index("space")

    def div(a, b):
        return lax.div(a, jnp.int32(b))

    def rem(a, b):
        return lax.rem(a, jnp.int32(b))

    zl, x = div(f, NX), rem(f, NX)
    zh, c = div(s, 8), rem(s, 2)
    y = div(rem(s, 8), 2)
    xr, xl, xo = rem(x + 1, NX), rem(x + 3, NX), rem(x + 2, NX)
    s_c = s + 1 - 2 * c
    s_n = rem(s + 15 + 2 * c, NS)
    s_h = rem(s + 8, NS)

    def at(zl_, x_, s_):
        return {"filter": zl_ * NX + x_, "space": s_}

    def lanes(start, size):
        return pl.ds(pl.multiple_of(start, 128), size)

    slots = Slots()
    pending = []

    def copy_to(src, dst, ss, rs, where):
        return pltpu.make_async_remote_copy(
            src_ref=src, dst_ref=dst, send_sem=sems.at[ss], recv_sem=sems.at[rs],
            device_id=where, device_id_type=MESH,
        )

    def send(src, dst, ss, rs, where):
        cp = copy_to(src, dst, ss, rs, where)
        cp.start()
        pending.append(cp)

    def recv(dst, rs, where):
        copy_to(dst, dst, rs, rs, where).wait_recv()

    barrier = pltpu.get_barrier_semaphore()
    peers = [at(rem(zl + t, NZ), x, s) for t in range(1, NZ)]
    peers += [at(rem(zl + t, NZ), x, s_h) for t in range(NZ)]
    peers += [at(zl, rem(x + t, NX), s) for t in range(1, NX)]
    peers += [at(zl, x, s_c), at(zl, x, s_n)]
    peers += [at(zl, x, zh * 8 + rem(y + t, NY) * 2 + c) for t in range(1, NY)]
    for peer in peers:
        pl.semaphore_signal(barrier, inc=1, device_id=peer, device_id_type=MESH)
    pl.semaphore_wait(barrier, len(peers))

    class Gather:
        def __init__(self, src, dst):
            self.src, self.dst = src, dst
            self.zs, self.zr = slots.take(NZ), slots.take(NZ)
            self.fs = [slots.take(NZ), slots.take(NZ)]
            self.fr = [slots.take(NZ), slots.take(NZ)]
            self.rs = [slots.take(NZ), slots.take(NZ)]
            self.rr = [slots.take(NZ), slots.take(NZ)]

        def forward(self, src, zf, t):
            send(src, self.dst.at[zf, x], self.fs[0] + t, self.fr[0] + t, at(zl, xr, s))
            send(src, self.dst.at[zf, x], self.fs[1] + t, self.fr[1] + t, at(zl, xl, s))

        def start(self):
            for t in ORDER:
                zt = rem(zl + t, NZ)
                send(self.src.at[:, lanes(PART * zt, PART)], self.dst.at[zl, x],
                     self.zs + t, self.zr + t, at(zt, x, s))
            self.forward(self.src.at[:, lanes(PART * zl, PART)], zl, 0)
            self.dst[zl, x] = self.src[:, lanes(PART * zl, PART)]

        def arrive(self, t):
            zf = rem(zl + NZ - t, NZ)
            recv(self.dst.at[zf, x], self.zr + t, at(zf, x, s))
            self.forward(self.dst.at[zf, x], zf, t)

        def relay(self, t):
            zf = rem(zl + NZ - t, NZ)
            low, high = pl.ds(0, HALF), pl.ds(HALF, HALF)
            recv(self.dst.at[zf, xl], self.fr[0] + t, at(zl, xl, s))
            part = self.dst.at[zf, xl, :, low]
            send(part, part, self.rs[0] + t, self.rr[0] + t, at(zl, xr, s))
            recv(self.dst.at[zf, xr], self.fr[1] + t, at(zl, xr, s))
            part = self.dst.at[zf, xr, :, high]
            send(part, part, self.rs[1] + t, self.rr[1] + t, at(zl, xl, s))

        def finish(self):
            for t in (0,) + ORDER:
                zf = rem(zl + NZ - t, NZ)
                recv(self.dst.at[zf, xo, :, pl.ds(0, HALF)], self.rr[0] + t, at(zl, xl, s))
                recv(self.dst.at[zf, xo, :, pl.ds(HALF, HALF)], self.rr[1] + t, at(zl, xr, s))

    class Scatter:
        def __init__(self, src, dst, offset):
            self.src, self.dst, self.offset = src, dst, offset
            self.ss, self.sr = slots.take(NZ), slots.take(NZ)

        def place(self, z):
            return self.dst.at[:, lanes(self.offset + PART * z, PART)]

        def start(self):
            for t in ORDER:
                zt = rem(zl + t, NZ)
                send(self.src.at[zt], self.place(zl), self.ss + t, self.sr + zl, at(zt, x, s))
            self.dst[:, lanes(self.offset + PART * zl, PART)] = self.src[zl]

        def wait(self, z):
            @pl.when(zl != z)
            def _():
                recv(self.place(z), self.sr + z, at(z, x, s))

    k = c * 4 + y
    own_cols = lanes(128 * k, 128)
    side = lanes(512 * c, 512)
    other = lanes(512 * (1 - c), 512)
    w1s, w1r = slots.take(NZ), slots.take(NZ)
    w2s, w2r = slots.take(NY), slots.take(NY)
    w3s, w3r = slots.take(1), slots.take(1)
    w4s, w4r = slots.take(NX), slots.take(NX)
    w5s, w5r = slots.take(NX), slots.take(NX)

    def space_y(t):
        return zh * 8 + rem(y + t, NY) * 2 + c

    def w1_start():
        for t in ORDER:
            send(mix.at[:, own_cols], wall.at[zl, x, :, own_cols], w1s + t, w1r + t, at(rem(zl + t, NZ), x, s))
        wall[zl, x, :, own_cols] = mix[:, own_cols]

    def w2_start():
        for t in ORDER:
            zf = rem(zl + NZ - t, NZ)
            recv(wall.at[zf, x, :, own_cols], w1r + t, at(zf, x, s))
        part = wall.at[:, x, :, own_cols]
        for t in range(1, NY):
            send(part, part, w2s + t, w2r + t, at(zl, x, space_y(t)))

    def w3_start():
        for t in range(1, NY):
            cols = lanes(128 * (c * 4 + rem(y + NY - t, NY)), 128)
            recv(wall.at[:, x, :, cols], w2r + t, at(zl, x, space_y(NY - t)))
        part = wall.at[:, x, :, side]
        send(part, part, w3s, w3r, at(zl, x, s_c))

    def w3_wait():
        recv(wall.at[:, x, :, other], w3r, at(zl, x, s_c))

    def w4_start():
        part = wall.at[:, x, :, side]
        for t in range(1, NX):
            send(part, part, w4s + t, w4r + t, at(zl, rem(x + t, NX), s))

    def w5_start():
        for t in range(1, NX):
            xf = rem(x + NX - t, NX)
            part = wall.at[:, xf, :, side]
            recv(part, w4r + t, at(zl, xf, s))
            send(part, part, w5s + t, w5r + t, at(zl, x, s_c))

    def w5_wait():
        for t in range(1, NX):
            xf = rem(x + NX - t, NX)
            recv(wall.at[:, xf, :, other], w5r + t, at(zl, x, s_c))

    lane = lax.broadcasted_iota(jnp.int32, (8, 8, 128), 2)
    first_col = lax.rem(lane, WW) == 0
    last_col = lax.rem(lane, WW) == WW - 1
    first_row = lane < WW
    zero = jnp.zeros((8, 8, 128), F32)

    def columns(v):
        before = jnp.where(first_col, zero, pltpu.roll(v, 1, 2))
        after = jnp.where(last_col, zero, pltpu.roll(v, 127, 2))
        return before, v, after

    def rows_down(v):
        swapped = pltpu.roll(v, WW, 2)
        above = jnp.concatenate([zero[:1], swapped[:-1]], axis=0)
        return jnp.where(first_row, above, swapped)

    def rows_up(v):
        swapped = pltpu.roll(v, WW, 2)
        below = jnp.concatenate([swapped[1:], zero[:1]], axis=0)
        return jnp.where(first_row, swapped, below)

    def conv(src, d, flip):
        @pl.loop(0, CH // 8)
        def _(g):
            rows = pl.ds(pl.multiple_of(8 * g, 8), 8)
            sums = [None] * 3
            for a in range(3):
                shifted = columns(src[pl.ds(8 * (d + a), 8), rows, :])
                for b in range(3):
                    for e in range(3):
                        tap = 9 * a + 3 * b + e
                        tap = 26 - tap if flip else tap
                        term = tb[tap, rows, :][None] * shifted[e]
                        sums[b] = term if sums[b] is None else sums[b] + term
            sp32[pl.ds(8 * d, 8), rows, :] = rows_down(sums[0]) + sums[1] + rows_up(sums[2])

    def widen(src, start, dst, chunk):
        for j in range(8):
            dst[chunk + j] = src[:, pl.ds(start + 128 * j, 128)].astype(F32)

    def pointwise(d):
        @pl.loop(0, 8)
        def _(j):
            at_chunk = 8 * d + j
            cells = lanes(128 * at_chunk, 128)
            spatial = sp32[at_chunk]
            sig = lax.logistic(spatial)
            grad = up[:, cells].astype(F32) * (sig * (1.0 + spatial * (1.0 - sig)))
            grad = grad.astype(BF16)
            sgb[:, cells] = grad
            sg32[8 + at_chunk] = grad.astype(F32)
            out[:, cells] = (vol[:, cells].astype(F32) + spatial * sig).astype(BF16)

    def forward_planes(first, step):
        @pl.loop(0, 2)
        def _(i):
            d = first + step * i
            conv(m32, d, False)
            pointwise(d)

    def backward_planes(first, step):
        @pl.loop(0, 2)
        def _(i):
            d = first + step * i
            conv(sg32, d, True)

            @pl.loop(0, 8)
            def _(j):
                mgb[:, lanes(128 * (8 * d + j), 128)] = sp32[8 * d + j].astype(BF16)

    def tap_sums():
        @pl.loop(0, CH // 8)
        def _(g):
            rows = pl.ds(pl.multiple_of(8 * g, 8), 8)
            for tap in range(27):
                tg[tap, rows, :] = zero[0]

            @pl.loop(0, PLANES)
            def _(d):
                grad = sg32[pl.ds(8 * d + 8, 8), rows, :]
                grads = (rows_up(grad), grad, rows_down(grad))
                for a in range(3):
                    shifted = columns(m32[pl.ds(8 * (d + a), 8), rows, :])
                    for b in range(3):
                        for e in range(3):
                            tap = 9 * a + 3 * b + e
                            tg[tap, rows, :] = tg[tap, rows, :] + jnp.sum(grads[b] * shifted[e], axis=0)

        tap_lane = lax.broadcasted_iota(jnp.int32, (CH, 128), 1)
        total = jnp.zeros((CH, 128), F32)
        for tap in range(27):
            total = jnp.where(tap_lane == tap, jnp.sum(tg[tap], axis=1, keepdims=True), total)
        ts[0] = total

    halo_s = [slots.take(2), slots.take(2)]
    halo_r = [slots.take(2), slots.take(2)]
    has_low, has_high = s > 0, s < NS - 1

    def halo_low(i, src, dst):
        return copy_to(src, dst, halo_s[i], halo_r[i], at(zl, x, s - 1))

    def halo_high(i, src, dst):
        return copy_to(src, dst, halo_s[i] + 1, halo_r[i] + 1, at(zl, x, s + 1))

    def m_low():
        return halo_low(0, mb.at[:, pl.ds(CELLS, CELLS)], mb.at[:, pl.ds(5 * CELLS, CELLS)])

    def m_high():
        return halo_high(0, mb.at[:, pl.ds(4 * CELLS, CELLS)], mb.at[:, pl.ds(0, CELLS)])

    def g_low():
        return halo_low(1, sgb.at[:, pl.ds(0, CELLS)], sgh.at[:, pl.ds(CELLS, CELLS)])

    def g_high():
        return halo_high(1, sgb.at[:, pl.ds(3 * CELLS, CELLS)], sgh.at[:, pl.ds(0, CELLS)])

    def halo_arrive(i, low_ref, low_at, high_ref, high_at, dst):
        @pl.when(has_low)
        def _():
            recv(low_ref.at[:, pl.ds(low_at, CELLS)], halo_r[i] + 1, at(zl, x, s - 1))
            widen(low_ref, low_at, dst, 0)

        @pl.when(s == 0)
        def _():
            for j in range(8):
                dst[j] = jnp.zeros((CH, 128), F32)

        @pl.when(has_high)
        def _():
            recv(high_ref.at[:, pl.ds(high_at, CELLS)], halo_r[i], at(zl, x, s + 1))
            widen(high_ref, high_at, dst, 40)

        @pl.when(s == NS - 1)
        def _():
            for j in range(8):
                dst[40 + j] = jnp.zeros((CH, 128), F32)

    volume_gather = Gather(vol, vol_all)
    grad_gather = Gather(mgb, mg_all)
    mixed_scatter = Scatter(mq, mb, CELLS)
    back_scatter = Scatter(bq, bb, 0)

    w1_start()
    volume_gather.start()
    for tap in range(27):
        tb[tap] = jnp.broadcast_to(taps[:, tap : tap + 1], (CH, 128))
    hooks = {1: w2_start, 4: w3_start}
    volume_gather.relay(0)
    for i, t in enumerate(ORDER):
        volume_gather.arrive(t)
        if i in hooks:
            hooks[i]()
        if i:
            volume_gather.relay(ORDER[i - 1])
    volume_gather.relay(ORDER[-1])
    w3_wait()
    volume_gather.finish()
    columns_own = wall[:, pl.ds(x, 1), :, :].reshape(NZ * CH, C)
    mixed = jnp.dot(columns_own, vol_all[...].reshape(C, PART), preferred_element_type=F32)
    mq[...] = mixed.astype(BF16).reshape(NZ, CH, PART)
    mixed_scatter.start()
    w4_start()
    for z in (0, 1):
        mixed_scatter.wait(z)
    pl.when(has_low)(lambda: m_low().start())
    for z in (6, 7):
        mixed_scatter.wait(z)
    pl.when(has_high)(lambda: m_high().start())
    for z in (2, 3, 4, 5):
        mixed_scatter.wait(z)

    for d in range(PLANES):
        widen(mb, CELLS * (d + 1), m32, 8 * (d + 1))
    forward_planes(1, 1)
    halo_arrive(0, mb, 0, mb, 5 * CELLS, m32)
    forward_planes(0, 3)
    pl.when(has_low)(lambda: g_low().start())
    pl.when(has_high)(lambda: g_high().start())
    w5_start()

    backward_planes(1, 1)
    tap_sums()
    halo_arrive(1, sgh, 0, sgh, CELLS, sg32)
    backward_planes(0, 3)
    grad_gather.start()

    t1s, t1r = slots.take(1), slots.take(1)
    t2s, t2r = slots.take(NY), slots.take(NY)
    t3s, t3r = slots.take(1), slots.take(1)
    send(ts.at[0], tr.at[0], t1s, t1r, at(zl, x, s_c))

    def taps_y():
        recv(tr.at[0], t1r, at(zl, x, s_c))
        ts[1] = ts[0] + tr[0]
        for t in range(1, NY):
            send(ts.at[1], tr.at[1 + y], t2s + t, t2r + t, at(zl, x, space_y(t)))
        tr[1 + y] = ts[1]

    def taps_z():
        for t in range(1, NY):
            recv(tr.at[1 + rem(y + NY - t, NY)], t2r + t, at(zl, x, space_y(NY - t)))
        ts[2] = (tr[1] + tr[2]) + (tr[3] + tr[4])
        send(ts.at[2], tr.at[5], t3s, t3r, at(zl, x, s_h))

    w5_wait()
    for z in range(NZ):
        block = wall[:, :, :, pl.ds(128 * z, 128)].reshape(C, 128)
        wt[z] = block.T.reshape(NX, CH, C)

    hooks = {2: taps_y, 5: taps_z}
    grad_gather.relay(0)
    for i, t in enumerate(ORDER):
        grad_gather.arrive(t)
        if i in hooks:
            hooks[i]()
        if i:
            grad_gather.relay(ORDER[i - 1])
    grad_gather.relay(ORDER[-1])

    d1s, d1r = slots.take(1), slots.take(1)
    d2s, d2r = slots.take(2 * NY), slots.take(2 * NY)
    d3s, d3r = slots.take(NS), slots.take(NS)
    d4s_sem, d4r_sem = slots.take(1), slots.take(1)
    own_grad = mg_all[:, pl.ds(x, 1), :, :].reshape(NZ * CH, PART)
    for i in range(4):
        part = lax.dot_general(
            own_grad, vol_all[pl.ds(2 * i, 2)].reshape(C // 4, PART),
            (((1,), (1,)), ((), ())), preferred_element_type=F32,
        )
        dw[:, :, :, pl.ds(256 * i, 256)] = part.reshape(NZ, 2, CH // 2, C // 4)
    send(dw.at[:, 1 - c], d1, d1s, d1r, at(zl, x, s_c))

    grad_gather.finish()
    rows_own = wt[:, pl.ds(x, 1), :, :].reshape(NZ * CH, C)
    back = jnp.dot(rows_own, mg_all[...].reshape(C, PART), preferred_element_type=F32)
    bq[...] = back.astype(BF16).reshape(NZ, CH, PART)
    back_scatter.start()

    recv(d1, d1r, at(zl, x, s_c))
    summed = d1[...] + dw[:, pl.ds(c, 1)].reshape(NZ, CH // 2, C)
    d1[...] = summed
    a1b[...] = summed.astype(BF16)
    for t in range(1, NY):
        for h in range(2):
            cols = lanes(128 * (4 * h + rem(y + t, NY)), 128)
            send(a1b.at[:, :, cols], d2.at[t - 1, h], d2s + 2 * t + h, d2r + 2 * t + h, at(zl, x, space_y(t)))
    for h in range(2):
        summed = d1[:, :, lanes(128 * (4 * h + y), 128)]
        for t in range(1, NY):
            recv(d2.at[t - 1, h], d2r + 2 * t + h, at(zl, x, space_y(NY - t)))
            summed = summed + d2[t - 1, h].astype(F32)
        a2[h] = summed
        a2b[h] = summed.astype(BF16)
    z_own = zh * NZ + zl

    def ring(t):
        z = rem(z_own + t, NS)
        return div(z, NZ), rem(z, NZ)

    for t in (8, 7, 9, 6, 10, 5, 11, 4, 12, 3, 13, 2, 14, 1, 15):
        h, z = ring(t)
        send(a2b.at[h, z], d3.at[t - 1], d3s + t, d3r + t, at(z, x, h * 8 + y * 2 + c))
    total = a2[zh, zl]
    for t in range(1, NS):
        h, z = ring(NS - t)
        recv(d3.at[t - 1], d3r + t, at(z, x, h * 8 + y * 2 + c))
        total = total + d3[t - 1].astype(F32)
    d4s[...] = total
    send(d4s, d4r, d4s_sem, d4r_sem, at(zl, x, s_c))

    for z in range(NZ):
        back_scatter.wait(z)

    @pl.loop(0, SLAB // 128)
    def _(j):
        cells = lanes(128 * j, 128)
        vgrad[:, cells] = (up[:, cells].astype(F32) + bb[:, cells].astype(F32)).astype(BF16)

    recv(tr.at[5], t3r, at(zl, x, s_h))
    tgrad[...] = ((ts[2] + tr[5]) * norm)[:, :27]
    recv(d4r, d4r_sem, at(zl, x, s_c))
    even = c == 0
    full = jnp.concatenate(
        [jnp.where(even, d4s[...], d4r[...]), jnp.where(even, d4r[...], d4s[...])], axis=0
    )
    mgrad[...] = jnp.where(even, full[:, :64], full[:, 64:]) * norm

    for cp in pending:
        cp.wait_send()
    for low, high in ((m_low, m_high), (g_low, g_high)):
        pl.when(has_low)(lambda low=low: low().wait_send())
        pl.when(has_high)(lambda high=high: high().wait_send())
    assert slots.used <= N_SEMS


def body(volume, mixing, kernel_taps, upstream):
    norm = 1.0 / math.sqrt(PLANES * NS * CELLS)
    vmem = pl.BlockSpec(memory_space=pltpu.VMEM)
    scratch = [
        ((NZ, NX, CH, PART), BF16),
        ((NZ, NX, CH, PART), BF16),
        ((NZ, NX, CH, C), BF16),
        ((NZ, NX, CH, C), BF16),
        ((NZ, CH, PART), BF16),
        ((NZ, CH, PART), BF16),
        ((CH, 6 * CELLS), BF16),
        ((48, CH, 128), F32),
        ((48, CH, 128), F32),
        ((32, CH, 128), F32),
        ((CH, SLAB), BF16),
        ((CH, 2 * CELLS), BF16),
        ((CH, SLAB), BF16),
        ((CH, SLAB), BF16),
        ((27, CH, 128), F32),
        ((27, CH, 128), F32),
        ((3, CH, 128), F32),
        ((6, CH, 128), F32),
        ((NZ, 2, CH // 2, C), F32),
        ((NZ, CH // 2, C), F32),
        ((NZ, CH // 2, C), BF16),
        ((3, 2, NZ, CH // 2, 128), BF16),
        ((2, NZ, CH // 2, 128), F32),
        ((2, NZ, CH // 2, 128), BF16),
        ((NS - 1, CH // 2, 128), BF16),
        ((CH // 2, 128), F32),
        ((CH // 2, 128), F32),
    ]
    output, volume_grad, mixing_grad, taps_grad = pl.pallas_call(
        functools.partial(kernel, norm),
        out_shape=(
            jax.ShapeDtypeStruct((CH, SLAB), BF16),
            jax.ShapeDtypeStruct((CH, SLAB), BF16),
            jax.ShapeDtypeStruct((CH, C // NS), F32),
            jax.ShapeDtypeStruct((CH, 27), F32),
        ),
        in_specs=[vmem] * 4,
        out_specs=(vmem,) * 4,
        scratch_shapes=[pltpu.VMEM(*one) for one in scratch] + [pltpu.SemaphoreType.DMA((N_SEMS,))],
        compiler_params=pltpu.CompilerParams(collective_id=0, has_side_effects=True),
        name="conv_block",
    )(volume.reshape(CH, SLAB), upstream.reshape(CH, SLAB), mixing, kernel_taps)
    shape = (CH, PLANES, CELLS)
    return output.reshape(shape), volume_grad.reshape(shape), mixing_grad, taps_grad


def solution(mesh):
    channel_slab = P("filter", "space", None)
    return jax.shard_map(
        body,
        mesh=mesh,
        in_specs=(channel_slab, P("filter", None), P("filter", None), channel_slab),
        out_specs=(channel_slab, channel_slab, P("filter", "space"), P("filter", None)),
        check_vma=False,
    )
```

time: 668 us -> 126 us (0.19)
  the two profiles are of different devices: /device:TPU:8 before, /device:TPU:1 now
where the time goes in v1:
time: 126 us
  Pallas kernels  119 us (94%)
  local copies, waits for them, and re-layouts  6.67 us (5%)
    pallas_call x1, Pallas kernels, body(): pl.pallas_call(functools.partial(kernel, norm), out_shape=(jax.ShapeDtype...  119 us
    unnamed x12, local copies, waits for them, and re-layouts  3.9 us

profile of v1, /device:TPU:1, one launch (start us, length us, event | category | flops | bytes accessed | tf_op | source)
XLA Modules:
  0.0 126.1 jit_solution(3814301871240768170)
XLA Ops:
  0.6 0.0 copy-start
  0.6 1.8 %copy.8 = bf16[4,8,4,1024]{3,1,2,0:T(8,128)(2,1)} copy(bf16[4,8,4,1024]{3,2,1,0:T(4,128)(2,1)} %bitcast.6) | data formatting | bytes 524288
  2.4 0.0 copy-done
  2.4 0.8 copy.9
  3.2 118.8 %conv_block.1 = (bf16[32,4096]{1,0:T(8,128)(2,1)}, bf16[32,4096]{1,0:T(8,128)(2,1)}, f32[32,64]{1,0:T(8,128)}, f32[32,27]{1,0:T(8,128)}) custom-call(bf16[32,4096]{1,0:T(8,128)(2,1)} %bitcast.4, bf16[32,4096]{1,0:T(8,128)(2,1)} %bitcast.5, bf16[32,1024]{1,0:T(8,128)(2,1)} %mix.1, f32[32,27]{1,0:T(8,128)} %taps.1), custom_call_target="tpu_custom_call" | custom-call | tf_op jit(solution)/shard_map/conv_block/pallas_call | solution.py:535
  122.0 0.0 copy-start.1
  122.0 1.9 %reshape.22 = bf16[32,4,1024]{2,1,0:T(4,128)(2,1)} reshape(bf16[32,4096]{1,0:T(8,128)(2,1)} %get-tuple-element.8) | data formatting | bytes 524288 | tf_op jit(solution)/shard_map/reshape | solution.py:550
  123.9 0.0 copy-done.1
  123.9 0.0 copy-start.3
  123.9 0.9 reshape.23
  124.8 0.0 copy-done.3
  124.8 0.0 copy-start.2
  124.8 0.6 copy.12
  125.4 0.1 copy-done.2
  125.5 0.6 copy.13
Async XLA Ops:
  0.6 1.8 %copy-start = (bf16[32,4,1024]{2,1,0:T(4,128)(2,1)S(1)}, bf16[32,4,1024]{2,1,0:T(4,128)(2,1)}, u32[]{:S(2)}) copy-start(bf16[32,4,1024]{2,1,0:T(4,128)(2,1)} %param.7) | copy-start | bytes 786436
  122.0 1.9 %copy-start.1 = (bf16[32,4096]{1,0:T(8,128)(2,1)S(1)}, bf16[32,4096]{1,0:T(8,128)(2,1)}, u32[]{:S(2)}) copy-start(bf16[32,4096]{1,0:T(8,128)(2,1)} %get-tuple-element.9) | copy-start | bytes 786436
  123.9 0.9 copy-start.3
  124.8 0.7 copy-start.2

commit v2 on v1

--- a/solution.py
+++ b/solution.py
@@ -19,7 +19,8 @@
 SLAB = PLANES * CELLS
 PART = SLAB // NZ
 C = NF * CH
-HALF = PART // 2
+CHUNKS = 4
+WIDTH = PART // CHUNKS
 ORDER = (4, 3, 5, 2, 6, 1, 7)
 
 
@@ -33,7 +34,7 @@
         return first
 
 
-N_SEMS = 330
+N_SEMS = 440
 
 
 def kernel(
@@ -53,7 +54,6 @@
     zl, x = div(f, NX), rem(f, NX)
     zh, c = div(s, 8), rem(s, 2)
     y = div(rem(s, 8), 2)
-    xr, xl, xo = rem(x + 1, NX), rem(x + 3, NX), rem(x + 2, NX)
     s_c = s + 1 - 2 * c
     s_n = rem(s + 15 + 2 * c, NS)
     s_h = rem(s + 8, NS)
@@ -63,6 +63,9 @@
 
     def lanes(start, size):
         return pl.ds(pl.multiple_of(start, 128), size)
+
+    def chunk(j):
+        return pl.ds(WIDTH * j, WIDTH)
 
     slots = Slots()
     pending = []
@@ -94,63 +97,54 @@
     class Gather:
         def __init__(self, src, dst):
             self.src, self.dst = src, dst
-            self.zs, self.zr = slots.take(NZ), slots.take(NZ)
-            self.fs = [slots.take(NZ), slots.take(NZ)]
-            self.fr = [slots.take(NZ), slots.take(NZ)]
-            self.rs = [slots.take(NZ), slots.take(NZ)]
-            self.rr = [slots.take(NZ), slots.take(NZ)]
-
-        def forward(self, src, zf, t):
-            send(src, self.dst.at[zf, x], self.fs[0] + t, self.fr[0] + t, at(zl, xr, s))
-            send(src, self.dst.at[zf, x], self.fs[1] + t, self.fr[1] + t, at(zl, xl, s))
+            self.zs, self.zr = slots.take(NZ * CHUNKS), slots.take(NZ * CHUNKS)
+            self.xs, self.xr = slots.take(NX * CHUNKS), slots.take(NX * CHUNKS)
 
         def start(self):
+            for j in range(CHUNKS):
+                for t in ORDER:
+                    zt = rem(zl + t, NZ)
+                    send(self.src.at[:, lanes(PART * zt + WIDTH * j, WIDTH)], self.dst.at[zl, x, :, chunk(j)],
+                         self.zs + NZ * j + t, self.zr + NZ * j + t, at(zt, x, s))
+            self.dst[zl, x] = self.src[:, lanes(PART * zl, PART)]
+
+        def arrive(self, j):
             for t in ORDER:
-                zt = rem(zl + t, NZ)
-                send(self.src.at[:, lanes(PART * zt, PART)], self.dst.at[zl, x],
-                     self.zs + t, self.zr + t, at(zt, x, s))
-            self.forward(self.src.at[:, lanes(PART * zl, PART)], zl, 0)
-            self.dst[zl, x] = self.src[:, lanes(PART * zl, PART)]
-
-        def arrive(self, t):
-            zf = rem(zl + NZ - t, NZ)
-            recv(self.dst.at[zf, x], self.zr + t, at(zf, x, s))
-            self.forward(self.dst.at[zf, x], zf, t)
-
-        def relay(self, t):
-            zf = rem(zl + NZ - t, NZ)
-            low, high = pl.ds(0, HALF), pl.ds(HALF, HALF)
-            recv(self.dst.at[zf, xl], self.fr[0] + t, at(zl, xl, s))
-            part = self.dst.at[zf, xl, :, low]
-            send(part, part, self.rs[0] + t, self.rr[0] + t, at(zl, xr, s))
-            recv(self.dst.at[zf, xr], self.fr[1] + t, at(zl, xr, s))
-            part = self.dst.at[zf, xr, :, high]
-            send(part, part, self.rs[1] + t, self.rr[1] + t, at(zl, xl, s))
-
-        def finish(self):
-            for t in (0,) + ORDER:
                 zf = rem(zl + NZ - t, NZ)
-                recv(self.dst.at[zf, xo, :, pl.ds(0, HALF)], self.rr[0] + t, at(zl, xl, s))
-                recv(self.dst.at[zf, xo, :, pl.ds(HALF, HALF)], self.rr[1] + t, at(zl, xr, s))
+                recv(self.dst.at[zf, x, :, chunk(j)], self.zr + NZ * j + t, at(zf, x, s))
+            part = self.dst.at[:, x, :, chunk(j)]
+            for t in (2, 1, 3):
+                send(part, part, self.xs + NX * j + t, self.xr + NX * j + t, at(zl, rem(x + t, NX), s))
+
+        def finish(self, j):
+            for t in (1, 3, 2):
+                xf = rem(x + NX - t, NX)
+                recv(self.dst.at[:, xf, :, chunk(j)], self.xr + NX * j + t, at(zl, xf, s))
 
     class Scatter:
         def __init__(self, src, dst, offset):
             self.src, self.dst, self.offset = src, dst, offset
-            self.ss, self.sr = slots.take(NZ), slots.take(NZ)
-
-        def place(self, z):
-            return self.dst.at[:, lanes(self.offset + PART * z, PART)]
-
-        def start(self):
+            self.ss, self.sr = slots.take(NZ * CHUNKS), slots.take(NZ * CHUNKS)
+
+        def place(self, z, j):
+            return self.dst.at[:, lanes(self.offset + PART * z + WIDTH * j, WIDTH)]
+
+        def start(self, j):
             for t in ORDER:
                 zt = rem(zl + t, NZ)
-                send(self.src.at[zt], self.place(zl), self.ss + t, self.sr + zl, at(zt, x, s))
-            self.dst[:, lanes(self.offset + PART * zl, PART)] = self.src[zl]
+                send(self.src.at[zt, :, chunk(j)], self.place(zl, j),
+                     self.ss + NZ * j + t, self.sr + NZ * j + zl, at(zt, x, s))
+            self.dst[:, lanes(self.offset + PART * zl + WIDTH * j, WIDTH)] = self.src[zl, :, chunk(j)]
 
         def wait(self, z):
             @pl.when(zl != z)
             def _():
-                recv(self.place(z), self.sr + z, at(z, x, s))
+                for j in range(CHUNKS):
+                    recv(self.place(z, j), self.sr + NZ * j + z, at(z, x, s))
+
+    def multiply(weights, data, j, dst):
+        product = jnp.dot(weights, data[:, :, :, chunk(j)].reshape(C, WIDTH), preferred_element_type=F32)
+        dst[:, :, chunk(j)] = product.astype(BF16).reshape(NZ, CH, WIDTH)
 
     k = c * 4 + y
     own_cols = lanes(128 * k, 128)
@@ -351,21 +345,17 @@
     volume_gather.start()
     for tap in range(27):
         tb[tap] = jnp.broadcast_to(taps[:, tap : tap + 1], (CH, 128))
-    hooks = {1: w2_start, 4: w3_start}
-    volume_gather.relay(0)
-    for i, t in enumerate(ORDER):
-        volume_gather.arrive(t)
-        if i in hooks:
-            hooks[i]()
-        if i:
-            volume_gather.relay(ORDER[i - 1])
-    volume_gather.relay(ORDER[-1])
+    w2_start()
+    for j in range(CHUNKS):
+        volume_gather.arrive(j)
+        if j == CHUNKS // 2:
+            w3_start()
     w3_wait()
-    volume_gather.finish()
     columns_own = wall[:, pl.ds(x, 1), :, :].reshape(NZ * CH, C)
-    mixed = jnp.dot(columns_own, vol_all[...].reshape(C, PART), preferred_element_type=F32)
-    mq[...] = mixed.astype(BF16).reshape(NZ, CH, PART)
-    mixed_scatter.start()
+    for j in range(CHUNKS):
+        volume_gather.finish(j)
+        multiply(columns_own, vol_all, j, mq)
+        mixed_scatter.start(j)
     w4_start()
     for z in (0, 1):
         mixed_scatter.wait(z)
@@ -414,15 +404,11 @@
         block = wall[:, :, :, pl.ds(128 * z, 128)].reshape(C, 128)
         wt[z] = block.T.reshape(NX, CH, C)
 
-    hooks = {2: taps_y, 5: taps_z}
-    grad_gather.relay(0)
-    for i, t in enumerate(ORDER):
-        grad_gather.arrive(t)
-        if i in hooks:
-            hooks[i]()
-        if i:
-            grad_gather.relay(ORDER[i - 1])
-    grad_gather.relay(ORDER[-1])
+    for j in range(CHUNKS):
+        grad_gather.arrive(j)
+        if j == 0:
+            taps_y()
+    taps_z()
 
     d1s, d1r = slots.take(1), slots.take(1)
     d2s, d2r = slots.take(2 * NY), slots.take(2 * NY)
@@ -437,12 +423,14 @@
         dw[:, :, :, pl.ds(256 * i, 256)] = part.reshape(NZ, 2, CH // 2, C // 4)
     send(dw.at[:, 1 - c], d1, d1s, d1r, at(zl, x, s_c))
 
-    grad_gather.finish()
     rows_own = wt[:, pl.ds(x, 1), :, :].reshape(NZ * CH, C)
-    back = jnp.dot(rows_own, mg_all[...].reshape(C, PART), preferred_element_type=F32)
-    bq[...] = back.astype(BF16).reshape(NZ, CH, PART)
-    back_scatter.start()
-
+
+    def back(j):
+        grad_gather.finish(j)
+        multiply(rows_own, mg_all, j, bq)
+        back_scatter.start(j)
+
+    back(0)
     recv(d1, d1r, at(zl, x, s_c))
     summed = d1[...] + dw[:, pl.ds(c, 1)].reshape(NZ, CH // 2, C)
     d1[...] = summed
@@ -451,6 +439,8 @@
         for h in range(2):
             cols = lanes(128 * (4 * h + rem(y + t, NY)), 128)
             send(a1b.at[:, :, cols], d2.at[t - 1, h], d2s + 2 * t + h, d2r + 2 * t + h, at(zl, x, space_y(t)))
+    for j in range(1, CHUNKS):
+        back(j)
     for h in range(2):
         summed = d1[:, :, lanes(128 * (4 * h + y), 128)]
         for t in range(1, NY):
@@ -497,7 +487,7 @@
     for low, high in ((m_low, m_high), (g_low, g_high)):
         pl.when(has_low)(lambda low=low: low().wait_send())
         pl.when(has_high)(lambda high=high: high().wait_send())
-    assert slots.used <= N_SEMS
+    assert slots.used <= N_SEMS, slots.used
 
 
 def body(volume, mixing, kernel_taps, upstream):

time: 126 us -> 111 us (0.88)
  Pallas kernels: 119 us -> 103 us
    pallas_call x1, Pallas kernels: 119 us -> 103 us  [body(): pl.pallas_call(functools.partial(kernel, norm), out_shape=(jax.ShapeDtype...]
where the time goes in v2:
time: 111 us
  Pallas kernels  103 us (93%)
  local copies, waits for them, and re-layouts  6.67 us (6%)
    pallas_call x1, Pallas kernels, body(): pl.pallas_call(functools.partial(kernel, norm), out_shape=(jax.ShapeDtype...  103 us
    unnamed x12, local copies, waits for them, and re-layouts  3.9 us

profile of v2, /device:TPU:1, one launch (start us, length us, event | category | flops | bytes accessed | tf_op | source)
XLA Modules:
  0.0 110.7 jit_solution(6998545363545845964)
XLA Ops:
  0.6 0.0 copy-start
  0.6 1.8 %copy.8 = bf16[4,8,4,1024]{3,1,2,0:T(8,128)(2,1)} copy(bf16[4,8,4,1024]{3,2,1,0:T(4,128)(2,1)} %bitcast.6) | data formatting | bytes 524288
  2.4 0.0 copy-done
  2.4 0.8 copy.9
  3.2 103.4 %conv_block.1 = (bf16[32,4096]{1,0:T(8,128)(2,1)}, bf16[32,4096]{1,0:T(8,128)(2,1)}, f32[32,64]{1,0:T(8,128)}, f32[32,27]{1,0:T(8,128)}) custom-call(bf16[32,4096]{1,0:T(8,128)(2,1)} %bitcast.4, bf16[32,4096]{1,0:T(8,128)(2,1)} %bitcast.5, bf16[32,1024]{1,0:T(8,128)(2,1)} %mix.1, f32[32,27]{1,0:T(8,128)} %taps.1), custom_call_target="tpu_custom_call" | custom-call | tf_op jit(solution)/shard_map/conv_block/pallas_call | solution.py:525
  106.6 0.0 copy-start.1
  106.6 1.9 %reshape.22 = bf16[32,4,1024]{2,1,0:T(4,128)(2,1)} reshape(bf16[32,4096]{1,0:T(8,128)(2,1)} %get-tuple-element.8) | data formatting | bytes 524288 | tf_op jit(solution)/shard_map/reshape | solution.py:540
  108.5 0.0 copy-done.1
  108.5 0.0 copy-start.3
  108.5 0.9 reshape.23
  109.3 0.0 copy-done.3
  109.3 0.0 copy-start.2
  109.3 0.6 copy.12
  110.0 0.1 copy-done.2
  110.1 0.6 copy.13
Async XLA Ops:
  0.6 1.8 %copy-start = (bf16[32,4,1024]{2,1,0:T(4,128)(2,1)S(1)}, bf16[32,4,1024]{2,1,0:T(4,128)(2,1)}, u32[]{:S(2)}) copy-start(bf16[32,4,1024]{2,1,0:T(4,128)(2,1)} %param.7) | copy-start | bytes 786436
  106.6 1.9 %copy-start.1 = (bf16[32,4096]{1,0:T(8,128)(2,1)S(1)}, bf16[32,4096]{1,0:T(8,128)(2,1)}, u32[]{:S(2)}) copy-start(bf16[32,4096]{1,0:T(8,128)(2,1)} %get-tuple-element.9) | copy-start | bytes 786436
  108.5 0.9 copy-start.3
  109.3 0.7 copy-start.2

commit v3 on v2

--- a/solution.py
+++ b/solution.py
@@ -34,12 +34,12 @@
         return first
 
 
-N_SEMS = 440
+N_SEMS = 480
 
 
 def kernel(
-    norm, vol, up, mix, taps, out, vgrad, mgrad, tgrad,
-    vol_all, mg_all, wall, wt, mq, bq, mb, m32, sg32, sp32, sgb, sgh, mgb, bb, tb, tg, ts, tr,
+    norm, vol_planes, up_planes, mix, taps, out, vgrad, mgrad, tgrad,
+    vol, up, vol_all, mg_all, wall, wt, mq, bq, mb, m32, sg32, sp32, sgb, sgh, mgb, bb, tb, tg, ts, tr,
     dw, d1, a1b, d2, a2, a2b, d3, d4s, d4r, sems,
 ):
     f = lax.axis_index("filter")
@@ -92,7 +92,26 @@
     peers += [at(zl, x, zh * 8 + rem(y + t, NY) * 2 + c) for t in range(1, NY)]
     for peer in peers:
         pl.semaphore_signal(barrier, inc=1, device_id=peer, device_id_type=MESH)
-    pl.semaphore_wait(barrier, len(peers))
+
+    crossing = (s == 7) | (s == 8)
+
+    @pl.when(crossing)
+    def _():
+        for z in range(NZ):
+            pl.semaphore_signal(barrier, inc=1, device_id=at(z, x, 15 - s), device_id_type=MESH)
+
+    for i in range(0, CH, 8):
+        rows = pl.ds(i, 8)
+        vol[rows] = (lambda v: v.reshape(8, SLAB))(vol_planes[rows])
+        up[rows] = (lambda v: v.reshape(8, SLAB))(up_planes[rows])
+
+    @pl.when(crossing)
+    def _():
+        pl.semaphore_wait(barrier, len(peers) + NZ)
+
+    @pl.when((s < 7) | (s > 8))
+    def _():
+        pl.semaphore_wait(barrier, len(peers))
 
     class Gather:
         def __init__(self, src, dst):
@@ -108,10 +127,13 @@
                          self.zs + NZ * j + t, self.zr + NZ * j + t, at(zt, x, s))
             self.dst[zl, x] = self.src[:, lanes(PART * zl, PART)]
 
-        def arrive(self, j):
+        def take(self, j):
             for t in ORDER:
                 zf = rem(zl + NZ - t, NZ)
                 recv(self.dst.at[zf, x, :, chunk(j)], self.zr + NZ * j + t, at(zf, x, s))
+
+        def arrive(self, j):
+            self.take(j)
             part = self.dst.at[:, x, :, chunk(j)]
             for t in (2, 1, 3):
                 send(part, part, self.xs + NX * j + t, self.xr + NX * j + t, at(zl, rem(x + t, NX), s))
@@ -120,6 +142,32 @@
             for t in (1, 3, 2):
                 xf = rem(x + NX - t, NX)
                 recv(self.dst.at[:, xf, :, chunk(j)], self.xr + NX * j + t, at(zl, xf, s))
+
+    class PlaneGather(Gather):
+        def piece(self, q, j):
+            return copy_to(self.src.at[:, pl.ds(PART * q + WIDTH * j, WIDTH)], self.dst.at[zl, x, :, chunk(j)],
+                           self.zs + NZ * j + q, self.zr + NZ * j + zl, at(q, x, s))
+
+        def start(self, parts):
+            for j in range(CHUNKS):
+                for q in parts:
+                    pl.when(zl != q)(lambda: self.piece(q, j).start())
+
+        def own(self):
+            self.dst[zl, x] = self.src[:, lanes(PART * zl, PART)]
+
+        def take(self, j):
+            for z in range(NZ):
+                @pl.when(zl != z)
+                def _():
+                    recv(self.dst.at[z, x, :, chunk(j)], self.zr + NZ * j + z, at(z, x, s))
+
+        def drain(self):
+            for q in range(NZ):
+                @pl.when(zl != q)
+                def _():
+                    for j in range(CHUNKS):
+                        self.piece(q, j).wait_send()
 
     class Scatter:
         def __init__(self, src, dst, offset):
@@ -252,8 +300,8 @@
             sg32[8 + at_chunk] = grad.astype(F32)
             out[:, cells] = (vol[:, cells].astype(F32) + spatial * sig).astype(BF16)
 
-    def forward_planes(first, step):
-        @pl.loop(0, 2)
+    def forward_planes(first, step, count):
+        @pl.loop(0, count)
         def _(i):
             d = first + step * i
             conv(m32, d, False)
@@ -296,6 +344,7 @@
     halo_s = [slots.take(2), slots.take(2)]
     halo_r = [slots.take(2), slots.take(2)]
     has_low, has_high = s > 0, s < NS - 1
+    sends_low, sends_high = (s > 0) & (s != 8), (s < NS - 1) & (s != 7)
 
     def halo_low(i, src, dst):
         return copy_to(src, dst, halo_s[i], halo_r[i], at(zl, x, s - 1))
@@ -314,6 +363,49 @@
 
     def g_high():
         return halo_high(1, sgb.at[:, pl.ds(3 * CELLS, CELLS)], sgh.at[:, pl.ds(0, CELLS)])
+
+    cross_s, cross_r = slots.take(NZ * CHUNKS), slots.take(2 * CHUNKS)
+    cross_part = zl - 6 * (8 - s)
+    cross_sends = ((s == 7) & (zl >= 6)) | ((s == 8) & (zl <= 1))
+
+    def cross_copy(z, j):
+        place = mb.at[:, lanes(5 * CELLS * (s - 7) + PART * cross_part + WIDTH * j, WIDTH)]
+        return copy_to(mq.at[z, :, chunk(j)], place, cross_s + NZ * j + z,
+                       cross_r + CHUNKS * cross_part + j, at(z, x, 15 - s))
+
+    def cross_start(j):
+        @pl.when(cross_sends)
+        def _():
+            for z in range(NZ):
+                cross_copy(z, j).start()
+
+    def cross_arrive(start, first_z):
+        for part in range(2):
+            for j in range(CHUNKS):
+                recv(mb.at[:, pl.ds(start + PART * part + WIDTH * j, WIDTH)],
+                     cross_r + CHUNKS * part + j, at(first_z + part, x, 15 - s))
+
+    def mixed_halo_arrive():
+        @pl.when((s > 0) & (s != 8))
+        def _():
+            recv(mb.at[:, pl.ds(0, CELLS)], halo_r[0] + 1, at(zl, x, s - 1))
+
+        pl.when(s == 8)(lambda: cross_arrive(0, 6))
+
+        @pl.when((s < NS - 1) & (s != 7))
+        def _():
+            recv(mb.at[:, pl.ds(5 * CELLS, CELLS)], halo_r[0], at(zl, x, s + 1))
+
+        pl.when(s == 7)(lambda: cross_arrive(5 * CELLS, 0))
+        for edge, start, row in ((s == 0, 0, 0), (s == NS - 1, 5 * CELLS, 40)):
+            @pl.when(edge)
+            def _():
+                for j in range(8):
+                    m32[row + j] = jnp.zeros((CH, 128), F32)
+
+            @pl.when(jnp.logical_not(edge))
+            def _():
+                widen(mb, start, m32, row)
 
     def halo_arrive(i, low_ref, low_at, high_ref, high_at, dst):
         @pl.when(has_low)
@@ -337,7 +429,7 @@
                 dst[40 + j] = jnp.zeros((CH, 128), F32)
 
     volume_gather = Gather(vol, vol_all)
-    grad_gather = Gather(mgb, mg_all)
+    grad_gather = PlaneGather(mgb, mg_all)
     mixed_scatter = Scatter(mq, mb, CELLS)
     back_scatter = Scatter(bq, bb, 0)
 
@@ -356,30 +448,34 @@
         volume_gather.finish(j)
         multiply(columns_own, vol_all, j, mq)
         mixed_scatter.start(j)
+        cross_start(j)
     w4_start()
     for z in (0, 1):
         mixed_scatter.wait(z)
-    pl.when(has_low)(lambda: m_low().start())
+    pl.when(sends_low)(lambda: m_low().start())
     for z in (6, 7):
         mixed_scatter.wait(z)
-    pl.when(has_high)(lambda: m_high().start())
+    pl.when(sends_high)(lambda: m_high().start())
     for z in (2, 3, 4, 5):
         mixed_scatter.wait(z)
 
     for d in range(PLANES):
         widen(mb, CELLS * (d + 1), m32, 8 * (d + 1))
-    forward_planes(1, 1)
-    halo_arrive(0, mb, 0, mb, 5 * CELLS, m32)
-    forward_planes(0, 3)
+    forward_planes(1, 1, 1)
+    mixed_halo_arrive()
+    forward_planes(0, 3, 2)
     pl.when(has_low)(lambda: g_low().start())
     pl.when(has_high)(lambda: g_high().start())
     w5_start()
 
+    forward_planes(2, 1, 1)
     backward_planes(1, 1)
+    grad_gather.start((3, 4, 2, 5))
     tap_sums()
     halo_arrive(1, sgh, 0, sgh, CELLS, sg32)
     backward_planes(0, 3)
-    grad_gather.start()
+    grad_gather.start((0, 7, 1, 6))
+    grad_gather.own()
 
     t1s, t1r = slots.take(1), slots.take(1)
     t2s, t2r = slots.take(NY), slots.take(NY)
@@ -484,9 +580,18 @@
 
     for cp in pending:
         cp.wait_send()
-    for low, high in ((m_low, m_high), (g_low, g_high)):
-        pl.when(has_low)(lambda low=low: low().wait_send())
-        pl.when(has_high)(lambda high=high: high().wait_send())
+    pl.when(sends_low)(lambda: m_low().wait_send())
+    pl.when(sends_high)(lambda: m_high().wait_send())
+    pl.when(has_low)(lambda: g_low().wait_send())
+    pl.when(has_high)(lambda: g_high().wait_send())
+    grad_gather.drain()
+
+    @pl.when(cross_sends)
+    def _():
+        for j in range(CHUNKS):
+            for z in range(NZ):
+                cross_copy(z, j).wait_send()
+
     assert slots.used <= N_SEMS, slots.used
 
 
@@ -494,6 +599,8 @@
     norm = 1.0 / math.sqrt(PLANES * NS * CELLS)
     vmem = pl.BlockSpec(memory_space=pltpu.VMEM)
     scratch = [
+        ((CH, SLAB), BF16),
+        ((CH, SLAB), BF16),
         ((NZ, NX, CH, PART), BF16),
         ((NZ, NX, CH, PART), BF16),
         ((NZ, NX, CH, C), BF16),
@@ -535,9 +642,28 @@
         scratch_shapes=[pltpu.VMEM(*one) for one in scratch] + [pltpu.SemaphoreType.DMA((N_SEMS,))],
         compiler_params=pltpu.CompilerParams(collective_id=0, has_side_effects=True),
         name="conv_block",
-    )(volume.reshape(CH, SLAB), upstream.reshape(CH, SLAB), mixing, kernel_taps)
-    shape = (CH, PLANES, CELLS)
-    return output.reshape(shape), volume_grad.reshape(shape), mixing_grad, taps_grad
+    )(volume, upstream, mixing, kernel_taps)
+
+    def finish(o_ref, v_ref, m_ref, t_ref, out, vgrad, mgrad, tgrad):
+        for i in range(0, CH, 8):
+            rows = pl.ds(i, 8)
+            out[rows] = (lambda v: v.reshape(8, PLANES, CELLS))(o_ref[rows])
+            vgrad[rows] = (lambda v: v.reshape(8, PLANES, CELLS))(v_ref[rows])
+        mgrad[...] = m_ref[...]
+        tgrad[...] = t_ref[...]
+
+    return pl.pallas_call(
+        finish,
+        out_shape=(
+            jax.ShapeDtypeStruct((CH, PLANES, CELLS), BF16),
+            jax.ShapeDtypeStruct((CH, PLANES, CELLS), BF16),
+            jax.ShapeDtypeStruct((CH, C // NS), F32),
+            jax.ShapeDtypeStruct((CH, 27), F32),
+        ),
+        in_specs=[vmem] * 4,
+        out_specs=(vmem,) * 4,
+        name="by_planes",
+    )(output, volume_grad, mixing_grad, taps_grad)
 
 
 def solution(mesh):

time: 111 us -> 102 us (0.919)
  local copies, waits for them, and re-layouts: 6.67 us -> 0 us
  Pallas kernels: 103 us -> 101 us
    unnamed x12 -> x0, local copies, waits for them, and re-layouts: 3.9 us -> none
    pallas_call x1, Pallas kernels: 103 us -> 99.6 us  [body(): pl.pallas_call(functools.partial(kernel, norm), out_shape=(jax.ShapeDtype...]
    reshape x2 -> x0, local copies, waits for them, and re-layouts: 2.76 us -> none  [the longest x1 1.88 us: body(): output.reshape(shape)]
    pallas_call x0 -> x1, Pallas kernels: none -> 1.89 us  [body(): pl.pallas_call(finish, out_shape=(jax.ShapeDtypeStruct((CH, PLANES, CELLS...]
where the time goes in v3:
time: 102 us
  Pallas kernels  101 us (99%)
    pallas_call x1, Pallas kernels, body(): pl.pallas_call(functools.partial(kernel, norm), out_shape=(jax.ShapeDtype...  99.6 us

profile of v3, /device:TPU:1, one launch (start us, length us, event | category | flops | bytes accessed | tf_op | source)
XLA Modules:
  0.0 102.1 jit_solution(17346749440576941871)
XLA Ops:
  0.6 99.6 %conv_block.1 = (bf16[32,4096]{1,0:T(8,128)(2,1)}, bf16[32,4096]{1,0:T(8,128)(2,1)}, f32[32,64]{1,0:T(8,128)}, f32[32,27]{1,0:T(8,128)}) custom-call(bf16[32,4,1024]{2,1,0:T(4,128)(2,1)} %vol_planes.1, bf16[32,4,1024]{2,1,0:T(4,128)(2,1)} %up_planes.1, bf16[32,1024]{1,0:T(8,128)(2,1)} %mix.1, f32[32,27]{1,0:T(8,128)} %taps.1), custom_call_target="tpu_custom_call" | custom-call | tf_op jit(solution)/shard_map/conv_block/pallas_call | solution.py:632
  100.2 1.9 %by_planes.1 = (bf16[32,4,1024]{2,1,0:T(4,128)(2,1)}, bf16[32,4,1024]{2,1,0:T(4,128)(2,1)}, f32[32,64]{1,0:T(8,128)}, f32[32,27]{1,0:T(8,128)}) custom-call(bf16[32,4096]{1,0:T(8,128)(2,1)} %get-tuple-element.8.o_ref, bf16[32,4096]{1,0:T(8,128)(2,1)} %get-tuple-element.9.v_ref, f32[32,64]{1,0:T(8,128)} %get-tuple-element.10.m_ref, ...), custom_call_target="tpu_custom_call" | custom-call | tf_op jit(solution)/shard_map/by_planes/pallas_call | solution.py:655

commit v4 on v3

--- a/solution.py
+++ b/solution.py
@@ -40,7 +40,7 @@
 def kernel(
     norm, vol_planes, up_planes, mix, taps, out, vgrad, mgrad, tgrad,
     vol, up, vol_all, mg_all, wall, wt, mq, bq, mb, m32, sg32, sp32, sgb, sgh, mgb, bb, tb, tg, ts, tr,
-    dw, d1, a1b, d2, a2, a2b, d3, d4s, d4r, sems,
+    dw, dwb, d1, d1b, a1b, d2, a2, a2b, d3, d4s, d4r, sems, token,
 ):
     f = lax.axis_index("filter")
     s = lax.axis_index("space")
@@ -55,7 +55,7 @@
     zh, c = div(s, 8), rem(s, 2)
     y = div(rem(s, 8), 2)
     s_c = s + 1 - 2 * c
-    s_n = rem(s + 15 + 2 * c, NS)
+    s_n = zh * 8 + rem(rem(s, 8) + 7 + 2 * c, 8)
     s_h = rem(s + 8, NS)
 
     def at(zl_, x_, s_):
@@ -86,32 +86,48 @@
 
     barrier = pltpu.get_barrier_semaphore()
     peers = [at(rem(zl + t, NZ), x, s) for t in range(1, NZ)]
-    peers += [at(rem(zl + t, NZ), x, s_h) for t in range(NZ)]
     peers += [at(zl, rem(x + t, NX), s) for t in range(1, NX)]
     peers += [at(zl, x, s_c), at(zl, x, s_n)]
     peers += [at(zl, x, zh * 8 + rem(y + t, NY) * 2 + c) for t in range(1, NY)]
     for peer in peers:
         pl.semaphore_signal(barrier, inc=1, device_id=peer, device_id_type=MESH)
 
-    crossing = (s == 7) | (s == 8)
-
-    @pl.when(crossing)
+    edge = ((zl == 0) & (zh == 0)) | ((zl == NZ - 1) & (zh == 1))
+    partner = at(NZ - 1 - zl, x, s_h)
+
+    @pl.when(edge)
     def _():
-        for z in range(NZ):
-            pl.semaphore_signal(barrier, inc=1, device_id=at(z, x, 15 - s), device_id_type=MESH)
+        pl.semaphore_signal(barrier, inc=1, device_id=partner, device_id_type=MESH)
 
     for i in range(0, CH, 8):
         rows = pl.ds(i, 8)
         vol[rows] = (lambda v: v.reshape(8, SLAB))(vol_planes[rows])
         up[rows] = (lambda v: v.reshape(8, SLAB))(up_planes[rows])
 
-    @pl.when(crossing)
+    def tell(i, where):
+        pl.semaphore_signal(token.at[i], inc=1, device_id=where, device_id_type=MESH)
+
+    @pl.when(edge)
     def _():
-        pl.semaphore_wait(barrier, len(peers) + NZ)
-
-    @pl.when((s < 7) | (s > 8))
+        pl.semaphore_wait(barrier, len(peers) + 1)
+        tell(0, partner)
+
+    @pl.when(jnp.logical_not(edge))
     def _():
         pl.semaphore_wait(barrier, len(peers))
+
+    def other_half_to_column():
+        @pl.when(edge)
+        def _():
+            pl.semaphore_wait(token.at[0], 1)
+            for t in range(1, NZ):
+                tell(0, at(rem(zl + t, NZ), x, s))
+
+    def other_half_known():
+        pl.when(jnp.logical_not(edge))(lambda: pl.semaphore_wait(token.at[0], 1))
+        pl.when(s == 0)(lambda: tell(1, at(zl, x, 7)))
+        pl.when(s == NS - 1)(lambda: tell(1, at(zl, x, 8)))
+        pl.when((s == 7) | (s == 8))(lambda: pl.semaphore_wait(token.at[1], 1))
 
     class Gather:
         def __init__(self, src, dst):
@@ -438,6 +454,7 @@
     for tap in range(27):
         tb[tap] = jnp.broadcast_to(taps[:, tap : tap + 1], (CH, 128))
     w2_start()
+    other_half_to_column()
     for j in range(CHUNKS):
         volume_gather.arrive(j)
         if j == CHUNKS // 2:
@@ -448,6 +465,8 @@
         volume_gather.finish(j)
         multiply(columns_own, vol_all, j, mq)
         mixed_scatter.start(j)
+        if j == 0:
+            other_half_known()
         cross_start(j)
     w4_start()
     for z in (0, 1):
@@ -496,15 +515,19 @@
         send(ts.at[2], tr.at[5], t3s, t3r, at(zl, x, s_h))
 
     w5_wait()
+    picked = lax.broadcasted_iota(jnp.int32, (CH, 128), 1) == (
+        lax.broadcasted_iota(jnp.int32, (CH, 128), 0) + CH * x
+    )
+    picks = jnp.where(picked, 1.0, 0.0).astype(BF16)
     for z in range(NZ):
         block = wall[:, :, :, pl.ds(128 * z, 128)].reshape(C, 128)
-        wt[z] = block.T.reshape(NX, CH, C)
+        rows = lax.dot_general(picks, block, (((1,), (1,)), ((), ())), preferred_element_type=F32)
+        wt[z] = rows.astype(BF16)
 
     for j in range(CHUNKS):
         grad_gather.arrive(j)
         if j == 0:
             taps_y()
-    taps_z()
 
     d1s, d1r = slots.take(1), slots.take(1)
     d2s, d2r = slots.take(2 * NY), slots.take(2 * NY)
@@ -516,10 +539,13 @@
             own_grad, vol_all[pl.ds(2 * i, 2)].reshape(C // 4, PART),
             (((1,), (1,)), ((), ())), preferred_element_type=F32,
         )
-        dw[:, :, :, pl.ds(256 * i, 256)] = part.reshape(NZ, 2, CH // 2, C // 4)
-    send(dw.at[:, 1 - c], d1, d1s, d1r, at(zl, x, s_c))
-
-    rows_own = wt[:, pl.ds(x, 1), :, :].reshape(NZ * CH, C)
+        part = part.reshape(NZ, 2, CH // 2, C // 4)
+        dw[:, :, :, pl.ds(256 * i, 256)] = part
+        dwb[:, :, :, pl.ds(256 * i, 256)] = part.astype(BF16)
+    send(dwb.at[:, 1 - c], d1b, d1s, d1r, at(zl, x, s_c))
+    taps_z()
+
+    rows_own = wt[...].reshape(NZ * CH, C)
 
     def back(j):
         grad_gather.finish(j)
@@ -527,16 +553,15 @@
         back_scatter.start(j)
 
     back(0)
-    recv(d1, d1r, at(zl, x, s_c))
-    summed = d1[...] + dw[:, pl.ds(c, 1)].reshape(NZ, CH // 2, C)
+    recv(d1b, d1r, at(zl, x, s_c))
+    summed = d1b[...].astype(F32) + dw[:, pl.ds(c, 1)].reshape(NZ, CH // 2, C)
     d1[...] = summed
     a1b[...] = summed.astype(BF16)
     for t in range(1, NY):
         for h in range(2):
             cols = lanes(128 * (4 * h + rem(y + t, NY)), 128)
             send(a1b.at[:, :, cols], d2.at[t - 1, h], d2s + 2 * t + h, d2r + 2 * t + h, at(zl, x, space_y(t)))
-    for j in range(1, CHUNKS):
-        back(j)
+    back(1)
     for h in range(2):
         summed = d1[:, :, lanes(128 * (4 * h + y), 128)]
         for t in range(1, NY):
@@ -553,6 +578,8 @@
     for t in (8, 7, 9, 6, 10, 5, 11, 4, 12, 3, 13, 2, 14, 1, 15):
         h, z = ring(t)
         send(a2b.at[h, z], d3.at[t - 1], d3s + t, d3r + t, at(z, x, h * 8 + y * 2 + c))
+    back(2)
+    back(3)
     total = a2[zh, zl]
     for t in range(1, NS):
         h, z = ring(NS - t)
@@ -604,7 +631,7 @@
         ((NZ, NX, CH, PART), BF16),
         ((NZ, NX, CH, PART), BF16),
         ((NZ, NX, CH, C), BF16),
-        ((NZ, NX, CH, C), BF16),
+        ((NZ, CH, C), BF16),
         ((NZ, CH, PART), BF16),
         ((NZ, CH, PART), BF16),
         ((CH, 6 * CELLS), BF16),
@@ -620,7 +647,9 @@
         ((3, CH, 128), F32),
         ((6, CH, 128), F32),
         ((NZ, 2, CH // 2, C), F32),
+        ((NZ, 2, CH // 2, C), BF16),
         ((NZ, CH // 2, C), F32),
+        ((NZ, CH // 2, C), BF16),
         ((NZ, CH // 2, C), BF16),
         ((3, 2, NZ, CH // 2, 128), BF16),
         ((2, NZ, CH // 2, 128), F32),
@@ -639,7 +668,7 @@
         ),
         in_specs=[vmem] * 4,
         out_specs=(vmem,) * 4,
-        scratch_shapes=[pltpu.VMEM(*one) for one in scratch] + [pltpu.SemaphoreType.DMA((N_SEMS,))],
+        scratch_shapes=[pltpu.VMEM(*one) for one in scratch] + [pltpu.SemaphoreType.DMA((N_SEMS,)), pltpu.SemaphoreType.REGULAR((2,))],
         compiler_params=pltpu.CompilerParams(collective_id=0, has_side_effects=True),
         name="conv_block",
     )(volume, upstream, mixing, kernel_taps)

time: 102 us -> 98.7 us (0.968)
  Pallas kernels: 101 us -> 97.9 us
    pallas_call x1, Pallas kernels: 99.6 us -> 96.1 us  [body(): pl.pallas_call(functools.partial(kernel, norm), out_shape=(jax.ShapeDtype...]
where the time goes in v4:
time: 98.7 us; the launch traced here: 98.6 us
  Pallas kernels  97.9 us (99%)
    pallas_call x1, Pallas kernels, body(): pl.pallas_call(functools.partial(kernel, norm), out_shape=(jax.ShapeDtype...  96.1 us

profile of v4, /device:TPU:1, one launch (start us, length us, event | category | flops | bytes accessed | tf_op | source)
XLA Modules:
  0.0 98.6 jit_solution(725996203120202045)
XLA Ops:
  0.6 96.1 %conv_block.1 = (bf16[32,4096]{1,0:T(8,128)(2,1)}, bf16[32,4096]{1,0:T(8,128)(2,1)}, f32[32,64]{1,0:T(8,128)}, f32[32,27]{1,0:T(8,128)}) custom-call(bf16[32,4,1024]{2,1,0:T(4,128)(2,1)} %vol_planes.1, bf16[32,4,1024]{2,1,0:T(4,128)(2,1)} %up_planes.1, bf16[32,1024]{1,0:T(8,128)(2,1)} %mix.1, f32[32,27]{1,0:T(8,128)} %taps.1), custom_call_target="tpu_custom_call" | custom-call | tf_op jit(solution)/shard_map/conv_block/pallas_call | solution.py:661
  96.7 1.9 %by_planes.1 = (bf16[32,4,1024]{2,1,0:T(4,128)(2,1)}, bf16[32,4,1024]{2,1,0:T(4,128)(2,1)}, f32[32,64]{1,0:T(8,128)}, f32[32,27]{1,0:T(8,128)}) custom-call(bf16[32,4096]{1,0:T(8,128)(2,1)} %get-tuple-element.8.o_ref, bf16[32,4096]{1,0:T(8,128)(2,1)} %get-tuple-element.9.v_ref, f32[32,64]{1,0:T(8,128)} %get-tuple-element.10.m_ref, ...), custom_call_target="tpu_custom_call" | custom-call | tf_op jit(solution)/shard_map/by_planes/pallas_call | solution.py:684

commit v5 on v4

--- a/solution.py
+++ b/solution.py
@@ -457,7 +457,7 @@
     other_half_to_column()
     for j in range(CHUNKS):
         volume_gather.arrive(j)
-        if j == CHUNKS // 2:
+        if j == 1:
             w3_start()
     w3_wait()
     columns_own = wall[:, pl.ds(x, 1), :, :].reshape(NZ * CH, C)

time: 98.7 us -> 98.1 us (level)
  no operation moved by 1% of the time
where the time goes in v5:
time: 98.1 us; the launch traced here: 97.9 us
  Pallas kernels  97.3 us (99%)
    pallas_call x1, Pallas kernels, body(): pl.pallas_call(functools.partial(kernel, norm), out_shape=(jax.ShapeDtype...  95.4 us

profile of v5, /device:TPU:1, one launch (start us, length us, event | category | flops | bytes accessed | tf_op | source)
XLA Modules:
  0.0 97.9 jit_solution(2759861530200036422)
XLA Ops:
  0.6 95.4 %conv_block.1 = (bf16[32,4096]{1,0:T(8,128)(2,1)}, bf16[32,4096]{1,0:T(8,128)(2,1)}, f32[32,64]{1,0:T(8,128)}, f32[32,27]{1,0:T(8,128)}) custom-call(bf16[32,4,1024]{2,1,0:T(4,128)(2,1)} %vol_planes.1, bf16[32,4,1024]{2,1,0:T(4,128)(2,1)} %up_planes.1, bf16[32,1024]{1,0:T(8,128)(2,1)} %mix.1, f32[32,27]{1,0:T(8,128)} %taps.1), custom_call_target="tpu_custom_call" | custom-call | tf_op jit(solution)/shard_map/conv_block/pallas_call | solution.py:661
  96.0 1.9 %by_planes.1 = (bf16[32,4,1024]{2,1,0:T(4,128)(2,1)}, bf16[32,4,1024]{2,1,0:T(4,128)(2,1)}, f32[32,64]{1,0:T(8,128)}, f32[32,27]{1,0:T(8,128)}) custom-call(bf16[32,4096]{1,0:T(8,128)(2,1)} %get-tuple-element.8.o_ref, bf16[32,4096]{1,0:T(8,128)(2,1)} %get-tuple-element.9.v_ref, f32[32,64]{1,0:T(8,128)} %get-tuple-element.10.m_ref, ...), custom_call_target="tpu_custom_call" | custom-call | tf_op jit(solution)/shard_map/by_planes/pallas_call | solution.py:684

commit v6 on v5

--- a/solution.py
+++ b/solution.py
@@ -491,29 +491,6 @@
     backward_planes(1, 1)
     grad_gather.start((3, 4, 2, 5))
     tap_sums()
-    halo_arrive(1, sgh, 0, sgh, CELLS, sg32)
-    backward_planes(0, 3)
-    grad_gather.start((0, 7, 1, 6))
-    grad_gather.own()
-
-    t1s, t1r = slots.take(1), slots.take(1)
-    t2s, t2r = slots.take(NY), slots.take(NY)
-    t3s, t3r = slots.take(1), slots.take(1)
-    send(ts.at[0], tr.at[0], t1s, t1r, at(zl, x, s_c))
-
-    def taps_y():
-        recv(tr.at[0], t1r, at(zl, x, s_c))
-        ts[1] = ts[0] + tr[0]
-        for t in range(1, NY):
-            send(ts.at[1], tr.at[1 + y], t2s + t, t2r + t, at(zl, x, space_y(t)))
-        tr[1 + y] = ts[1]
-
-    def taps_z():
-        for t in range(1, NY):
-            recv(tr.at[1 + rem(y + NY - t, NY)], t2r + t, at(zl, x, space_y(NY - t)))
-        ts[2] = (tr[1] + tr[2]) + (tr[3] + tr[4])
-        send(ts.at[2], tr.at[5], t3s, t3r, at(zl, x, s_h))
-
     w5_wait()
     picked = lax.broadcasted_iota(jnp.int32, (CH, 128), 1) == (
         lax.broadcasted_iota(jnp.int32, (CH, 128), 0) + CH * x
@@ -523,6 +500,29 @@
         block = wall[:, :, :, pl.ds(128 * z, 128)].reshape(C, 128)
         rows = lax.dot_general(picks, block, (((1,), (1,)), ((), ())), preferred_element_type=F32)
         wt[z] = rows.astype(BF16)
+
+    halo_arrive(1, sgh, 0, sgh, CELLS, sg32)
+    backward_planes(0, 3)
+    grad_gather.start((0, 7, 1, 6))
+    grad_gather.own()
+
+    t1s, t1r = slots.take(1), slots.take(1)
+    t2s, t2r = slots.take(NY), slots.take(NY)
+    t3s, t3r = slots.take(1), slots.take(1)
+    send(ts.at[0], tr.at[0], t1s, t1r, at(zl, x, s_c))
+
+    def taps_y():
+        recv(tr.at[0], t1r, at(zl, x, s_c))
+        ts[1] = ts[0] + tr[0]
+        for t in range(1, NY):
+            send(ts.at[1], tr.at[1 + y], t2s + t, t2r + t, at(zl, x, space_y(t)))
+        tr[1 + y] = ts[1]
+
+    def taps_z():
+        for t in range(1, NY):
+            recv(tr.at[1 + rem(y + NY - t, NY)], t2r + t, at(zl, x, space_y(NY - t)))
+        ts[2] = (tr[1] + tr[2]) + (tr[3] + tr[4])
+        send(ts.at[2], tr.at[5], t3s, t3r, at(zl, x, s_h))
 
     for j in range(CHUNKS):
         grad_gather.arrive(j)

time: 98.1 us -> 97.6 us (level)
  no operation moved by 1% of the time
where the time goes in v6:
time: 97.6 us; the launch traced here: 97.4 us
  Pallas kernels  96.8 us (99%)
    pallas_call x1, Pallas kernels, body(): pl.pallas_call(functools.partial(kernel, norm), out_shape=(jax.ShapeDtype...  94.9 us

profile of v6, /device:TPU:1, one launch (start us, length us, event | category | flops | bytes accessed | tf_op | source)
XLA Modules:
  0.0 97.4 jit_solution(11266956785498499266)
XLA Ops:
  0.6 94.9 %conv_block.1 = (bf16[32,4096]{1,0:T(8,128)(2,1)}, bf16[32,4096]{1,0:T(8,128)(2,1)}, f32[32,64]{1,0:T(8,128)}, f32[32,27]{1,0:T(8,128)}) custom-call(bf16[32,4,1024]{2,1,0:T(4,128)(2,1)} %vol_planes.1, bf16[32,4,1024]{2,1,0:T(4,128)(2,1)} %up_planes.1, bf16[32,1024]{1,0:T(8,128)(2,1)} %mix.1, f32[32,27]{1,0:T(8,128)} %taps.1), custom_call_target="tpu_custom_call" | custom-call | tf_op jit(solution)/shard_map/conv_block/pallas_call | solution.py:661
  95.5 1.9 %by_planes.1 = (bf16[32,4,1024]{2,1,0:T(4,128)(2,1)}, bf16[32,4,1024]{2,1,0:T(4,128)(2,1)}, f32[32,64]{1,0:T(8,128)}, f32[32,27]{1,0:T(8,128)}) custom-call(bf16[32,4096]{1,0:T(8,128)(2,1)} %get-tuple-element.8.o_ref, bf16[32,4096]{1,0:T(8,128)(2,1)} %get-tuple-element.9.v_ref, f32[32,64]{1,0:T(8,128)} %get-tuple-element.10.m_ref, ...), custom_call_target="tpu_custom_call" | custom-call | tf_op jit(solution)/shard_map/by_planes/pallas_call | solution.py:684
